TPU v7x, 32 devices: a whole 2x2x4 slice. The times are simulated.
32 devices in a mesh: rep: 4 (over x, core), fsdp: 8 (over z, y).
Axes of the slice: x: 2, y: 2, z: 4, core: 2. Of those that a mesh axis runs over, the one named last changes fastest.
Arguments:
- deltas: float32 [4, 1048576], P('rep', 'fsdp'), may hold values from -45 to 45
- noise_first: float32 [4, 1048576], P('rep', 'fsdp'), may hold values from 0 to 1
- params: float32 [1048576], P('fsdp'), may hold values from -6 to 6
- momentum: float32 [1048576], P('fsdp'), may hold values from -6 to 6
- noise_second: float32 [1048576], P('fsdp'), may hold values from 0 to 1
Outputs:
- new_params: float32 [1048576], P('fsdp')
- new_momentum: float32 [1048576], P('fsdp')
All inputs are finite; a program needn't handle non-finite values.
Results may differ from a plain program's by a relative error of at most 0.0003.
Values may be sent and summed in bfloat16 or wider, within the bound.
A program may use at most 64 MiB of HBM per device.

v0:
```python
import jax
import jax.numpy as jnp
import numpy as np
from jax import lax
from jax.sharding import PartitionSpec as P

BLOCK = 32
LEVELS = 8


power_list = np.array([2.0**k for k in range(-40, 12)], dtype=np.float32)
target_rms = 0.2
outer_rate = 0.7
outer_mu = 0.9


def quantize(values, jitter):
    initial = values.shape
    blocks = values.reshape(-1, BLOCK)
    shaken = jitter.reshape(-1, BLOCK)
    largest = jnp.max(jnp.abs(blocks), axis=1, keepdims=True)
    powers = jnp.asarray(power_list, values.dtype)[None, :]
    ceiling = jnp.max(
        jnp.where(powers < largest, 2.0 * powers, powers[:, :1]), axis=1, keepdims=True
    )
    scaled = blocks * (LEVELS / ceiling)
    lower = jnp.floor(scaled)
    bumped = jnp.where(scaled - lower > shaken, 1.0, 0.0).astype(values.dtype)
    return ((lower + bumped) * (ceiling / LEVELS)).reshape(initial)


def apply_update(outer_grad, params, momentum, mean_square):
    factor = target_rms / jnp.sqrt(mean_square + 1e-06)
    update = factor * outer_grad
    new_moment = outer_mu * momentum + update
    new_param = params - outer_rate * (update + outer_mu * new_moment)
    return (new_param, new_moment)


def local(deltas, noise_first, params, momentum, noise_second):
    own_terms = quantize(deltas[0], noise_first[0])
    param_len = params.shape[0]
    full_count = param_len * lax.axis_size("fsdp")
    summed = lax.psum(own_terms.astype(jnp.bfloat16), "rep").astype(jnp.float32)
    outer_grad = quantize(summed / lax.axis_size("rep"), noise_second)
    mean_square = lax.psum(jnp.sum(outer_grad * outer_grad), "fsdp") / full_count
    return apply_update(outer_grad, params, momentum, mean_square)


def solution(mesh):
    in_specs = (P("rep", "fsdp"), P("rep", "fsdp"), P("fsdp"), P("fsdp"), P("fsdp"))
    out_specs = (P("fsdp"), P("fsdp"))
    return jax.shard_map(local, mesh=mesh, in_specs=in_specs, out_specs=out_specs, check_vma=False)
```

profile of v0, /device:TPU:0, one launch (start us, length us, event | category | flops | bytes accessed | tf_op | source)
XLA Modules:
  0.0 87.7 jit_solution(13472866310690952050)
XLA Ops:
  7.2 0.0 all-reduce.2.cloned.1.call-start
  7.2 2.6 %abs_reduce_fusion = f32[131072]{0:T(1024)S(1)} fusion(f32[1,131072]{1,0:T(1,128)} %param.7), kind=kLoop, calls=%fused_computation.17 | loop fusion | flops 131072 | bytes 1048576 | tf_op jit(solution)/shard_map/abs | solution.py:21
  9.8 0.0 copy-start.3
  9.8 0.0 copy-start.4
  9.9 0.5 abs.17
  10.3 0.6 reduce_max.36
  10.9 0.0 copy-done.3
  11.0 0.0 copy-done.4
  11.0 0.2 select_reduce_fusion.1
  11.2 0.6 mul.74
  11.8 0.5 mul.75
  12.3 0.6 mul.77
  12.9 0.5 mul.78
  13.4 2.0 %fusion.2 = bf16[131072]{0:T(1024)(128)(2,1)} fusion(f32[131072]{0:T(1024)S(1)} %mul.78, f32[131072]{0:T(1024)} %bitcast.3, f32[131072]{0:T(1024)} %bitcast.2, f32[131072]{0:T(1024)S(1)} %mul.75), kind=kLoop, calls=%fused_computation.8 | loop fusion | flops 1048576 | bytes 2359296 | tf_op jit(solution)/shard_map/convert_element_type | solution.py:44
  15.4 0.0 all-reduce.2.cloned.1.call-update
  15.4 35.1 %all-reduce.2.cloned.1.call-done = bf16[131072]{0:T(1024)(128)(2,1)} async-done(((bf16[131072]{0:T(1024)(128)(2,1)}), bf16[131072]{0:T(1024)(128)(2,1)}) %all-reduce.2.cloned.1.call-update) | async-done | bytes 262160 | tf_op jit(solution)/shard_map/psum | solution.py:44
  50.6 1.0 %fusion.6 = f32[131072]{0:T(1024)S(1)} fusion(bf16[131072]{0:T(1024)(128)(2,1)} %all-reduce.2.cloned.1.call-done), kind=kLoop, calls=%fused_computation.16 | loop fusion | flops 393216 | bytes 786432 | tf_op jit(solution)/shard_map/abs | solution.py:21
  51.6 0.5 abs.19
  52.1 0.6 reduce_max.38
  52.7 0.2 select_reduce_fusion
  52.9 0.6 mul.81
  53.5 0.5 mul.82
  54.0 0.0 copy-start
  54.0 0.6 mul.84
  54.6 0.5 mul.85
  55.1 0.0 copy-done
  55.1 0.0 copy-start.1
  55.1 0.0 copy-start.2
  55.1 1.9 %multiply_reduce_fusion = (f32[]{:T(128)}, f32[131072]{0:T(1024)S(1)}) fusion(f32[131072]{0:T(1024)S(1)} %mul.85, f32[131072]{0:T(1024)} %param.11, f32[131072]{0:T(1024)S(1)} %mul.82, bf16[131072]{0:T(1024)(128)(2,1)S(1)} %copy-done), kind=kLoop, calls=%fused_computation.13 | loop fusion | flops 1441791 | bytes 2359300 | tf_op jit(solution)/shard_map/reduce_sum | solution.py:46
  57.0 22.0 %psum.15 = f32[]{:T(128)} all-reduce(f32[]{:T(128)} %get-tuple-element.4), channel_id=1, replica_groups=mesh['rep'=4,'fsdp'=8] {'fsdp'}, use_global_device_ids=true, to_apply=%region_6.7 | all-reduce | flops 1 | bytes 8 | tf_op jit(solution)/shard_map/psum | solution.py:46
  79.7 0.0 copy-done.1
  79.7 1.1 %multiply_subtract_fusion = (f32[131072]{0:T(1024)}, f32[131072]{0:T(1024)}) fusion(f32[131072]{0:T(1024)S(1)} %copy-done.1, f32[131072]{0:T(1024)S(1)} %get-tuple-element.5, f32[]{:T(128)S(6)} %div.41, f32[131072]{0:T(1024)S(1)} %copy-done.2), kind=kLoop, calls=%fused_computation.11 | loop fusion | flops 917504 | bytes 2621444 | tf_op jit(solution)/shard_map/sub | solution.py:36
  (3 shorter events, 0.0 us)
Async XLA Ops:
  7.2 43.4 %all-reduce.2.cloned.1.call-start = ((), (), s32[]{:S(2)}) async-start(), calls=%async_computation | async-start | bytes 524288 | tf_op jit(solution)/shard_map/psum | solution.py:44
  9.8 1.1 %copy-start.3 = (f32[52]{0:T(128)S(1)}, f32[52]{0:T(128)}, u32[]{:S(2)}) copy-start(f32[52]{0:T(128)} %constant.32) | copy-start | bytes 628
  9.8 1.1 %copy-start.4 = (f32[52]{0:T(128)S(1)}, f32[52]{0:T(128)}, u32[]{:S(2)}) copy-start(f32[52]{0:T(128)} %constant.29.clone) | copy-start | bytes 628
  54.0 1.1 %copy-start = (bf16[131072]{0:T(1024)(128)(2,1)S(1)}, bf16[131072]{0:T(1024)(128)(2,1)}, u32[]{:S(2)}) copy-start(bf16[131072]{0:T(1024)(128)(2,1)} %all-reduce.2.cloned.1.call-done) | copy-start | bytes 786436
  55.1 24.6 %copy-start.1 = (f32[131072]{0:T(1024)S(1)}, f32[131072]{0:T(1024)}, u32[]{:S(2)}) copy-start(f32[131072]{0:T(1024)} %param.9) | copy-start | bytes 1572868
  55.1 24.6 %copy-start.2 = (f32[131072]{0:T(1024)S(1)}, f32[131072]{0:T(1024)}, u32[]{:S(2)}) copy-start(f32[131072]{0:T(1024)} %param.10) | copy-start | bytes 1572868
Sparse Core Ops, SparseCore 0:
  15.6 34.9 all-reduce.1
where the time goes:
time: 87.9 us; the launch traced here: 87.7 us
  waiting for transfers between devices  35.2 us (40%)
  blocking collectives  22 us (25%)
  between operations  14.9 us (17%)
  other arithmetic  10.3 us (12%)
  local copies, waits for them, and re-layouts  5.3 us (6%)
    psum x1, waiting for transfers between devices, local(): summed = lax.psum(own_terms.astype(jnp.bfloat16), 'rep').astype(jnp.float32)  35.1 us
    psum x1, blocking collectives, local(): lax.psum(jnp.sum(outer_grad * outer_grad), 'fsdp') / full_count  22 us
    abs x2, other arithmetic, quantize(): largest = jnp.max(jnp.abs(blocks), axis=1, keepdims=True)  3.63 us
    mul x4, local copies, waits for them, and re-layouts, quantize(): scaled = blocks * (LEVELS / ceiling)  2.16 us
    mul x4, local copies, waits for them, and re-layouts, quantize(): return ((lower + bumped) * (ceiling / LEVELS)).reshape(initial)  2.16 us
    convert_element_type x1, other arithmetic, local(): summed = lax.psum(own_terms.astype(jnp.bfloat16), 'rep').astype(jnp.float32)  2.04 us
    reduce_sum x1, other arithmetic, local(): jnp.sum(outer_grad * outer_grad)  1.92 us
  transfers between devices with their start and end apart: 1, of which 1 were waited for; matrix products, arithmetic and copies ran while one was open for 0% of the time, Pallas kernels for 0%

commit v1 on v0

v1 whole, which is shorter than its diff:
```python
import functools

import jax
import jax.numpy as jnp
from jax import lax
from jax.experimental import pallas as pl
from jax.experimental.pallas import tpu as pltpu
from jax.sharding import PartitionSpec as P

MESH = pl.DeviceIdType.MESH
LANES = 128
BLOCK = 32
LEVELS = 8
SMALLEST = 2.0**-40
UNDER = 1.0 - 2.0**-24
target_rms = 0.2
outer_rate = 0.7
outer_mu = 0.9


def block_max(values):
    lane = lax.broadcasted_iota(jnp.int32, values.shape, 1)
    largest = jnp.abs(values)
    step = 1
    while step < BLOCK:
        ahead = pltpu.roll(largest, LANES - step, 1)
        behind = pltpu.roll(largest, step, 1)
        largest = jnp.maximum(largest, jnp.where((lane & step) != 0, behind, ahead))
        step *= 2
    return largest


def quantize(values, jitter):
    largest = jnp.maximum(block_max(values), SMALLEST)
    spread = (largest * UNDER) * ((2.0**24 + 2.0) / LEVELS)
    unit = spread - spread * UNDER
    magic = unit * (1.5 * 2.0**23)
    near = (values + magic) - magic
    lower = jnp.where(near > values, near - unit, near)
    return lower + jnp.where(values - lower > jitter * unit, unit, 0.0)


def kernel(reps, fsdps, chunks, x_hbm, u_hbm, p_hbm, m_hbm, w_hbm, newp_hbm, newm_hbm,
           xv, uv, wv, pv, mv, snd, own, got, pair, gmine, gother, sq,
           x_sem, u_sem, w_sem, p_sem, m_sem, op_sem, om_sem,
           s1, r1, s2, r2, s3, r3, s4, r4):
    rep, fsdp = lax.axis_index("rep"), lax.axis_index("fsdp")
    core, chip = lax.rem(rep, 2), rep // 2
    partner = rep + 1 - 2 * core
    chips, sources = reps // 2, 2 * fsdps
    half = xv.shape[1]
    rows = half // chunks
    me = fsdp * 2 + core

    def chip_peer(d):
        other = lax.rem(chip + d, chips)
        return other, (2 * other + core, fsdp)

    def sum_peer(d):
        other = lax.rem(me + d, sources)
        return other, (rep - core + lax.rem(other, 2), other // 2)

    barrier = pltpu.get_barrier_semaphore()
    for d in range(1, chips):
        pl.semaphore_signal(barrier, inc=1, device_id=chip_peer(d)[1], device_id_type=MESH)

    def greet(d, carry):
        pl.semaphore_signal(barrier, inc=1, device_id=sum_peer(d)[1], device_id_type=MESH)
        return carry

    lax.fori_loop(1, sources, greet, 0)

    starts = ((1 - core) * half, core * half)

    def piece(start, c):
        return pl.ds(pl.multiple_of(start + c * rows, rows), rows)

    def part(c):
        return pl.ds(c * rows, rows)

    x_in, u_in = {}, {}
    for s in (0, 1):
        for c in range(chunks):
            x_in[s, c] = pltpu.make_async_copy(
                x_hbm.at[piece(starts[s], c)], xv.at[s, part(c)], x_sem.at[s, c])
            u_in[s, c] = pltpu.make_async_copy(
                u_hbm.at[piece(starts[s], c)], uv.at[s, part(c)], u_sem.at[s, c])
            x_in[s, c].start()
            u_in[s, c].start()
    mine = pl.ds(pl.multiple_of(starts[1], half), half)
    w_in = pltpu.make_async_copy(w_hbm.at[mine], wv, w_sem)
    w_in.start()
    p_in, m_in = {}, {}
    for s in (1, 0):
        span = pl.ds(pl.multiple_of(starts[s], half), half)
        m_in[s] = pltpu.make_async_copy(m_hbm.at[span], mv.at[s], m_sem.at[s])
        p_in[s] = pltpu.make_async_copy(p_hbm.at[span], pv.at[s], p_sem.at[s])
        m_in[s].start()
        p_in[s].start()

    first = []
    for c in range(chunks):
        x_in[0, c].wait()
        u_in[0, c].wait()
        snd[part(c)] = quantize(xv[0, part(c)], uv[0, part(c)]).astype(jnp.bfloat16)
        if c == 0:
            pl.semaphore_wait(barrier, chips - 1 + sources - 1)
        copy = pltpu.make_async_remote_copy(
            snd.at[part(c)], got.at[part(c)], s1.at[c], r1.at[c],
            device_id=(partner, fsdp), device_id_type=MESH)
        copy.start()
        first.append(copy)
    for c in range(chunks):
        x_in[1, c].wait()
        u_in[1, c].wait()
        own[part(c)] = quantize(xv[1, part(c)], uv[1, part(c)])

    second = []
    for c in range(chunks):
        first[c].wait_recv()
        both = own[part(c)] + got[part(c)].astype(jnp.float32)
        pair[chip, part(c)] = both.astype(jnp.bfloat16)
        for d in range(1, chips):
            copy = pltpu.make_async_remote_copy(
                pair.at[chip, part(c)], pair.at[chip, part(c)],
                s2.at[d, c], r2.at[chip, c],
                device_id=chip_peer(d)[1], device_id_type=MESH)
            copy.start()
            second.append(copy)

    for s in (1, 0):
        m_in[s].wait()
        p_in[s].wait()
        pv[s] = pv[s] - (outer_rate * outer_mu * outer_mu) * mv[s]
        mv[s] = outer_mu * mv[s]

    w_in.wait()
    third = []
    squares = jnp.zeros((8, LANES), jnp.float32)
    for c in range(chunks):
        for d in range(1, chips):
            other, where = chip_peer(d)
            pltpu.make_async_remote_copy(
                pair.at[other, part(c)], pair.at[other, part(c)],
                s2.at[d, c], r2.at[other, c],
                device_id=where, device_id_type=MESH).wait_recv()
        total = pair[0, part(c)].astype(jnp.float32)
        for k in range(1, chips):
            total = total + pair[k, part(c)].astype(jnp.float32)
        grad = quantize(total / reps, wv[part(c)])
        gmine[part(c)] = grad.astype(jnp.bfloat16)
        copy = pltpu.make_async_remote_copy(
            gmine.at[part(c)], gother.at[part(c)], s3.at[c], r3.at[c],
            device_id=(partner, fsdp), device_id_type=MESH)
        copy.start()
        third.append(copy)
        squares = squares + jnp.sum((grad * grad).reshape(-1, 8, LANES), axis=0)

    sq[me] = jnp.sum(squares, axis=0, keepdims=True)

    def tell(d, carry):
        pltpu.make_async_remote_copy(
            sq.at[me], sq.at[me], s4.at[d], r4.at[me],
            device_id=sum_peer(d)[1], device_id_type=MESH).start()
        return carry

    lax.fori_loop(1, sources, tell, 0)

    def hear(d, carry):
        other, where = sum_peer(d)
        pltpu.make_async_remote_copy(
            sq.at[other], sq.at[other], s4.at[d], r4.at[other],
            device_id=where, device_id_type=MESH).wait_recv()
        return carry

    lax.fori_loop(1, sources, hear, 0)
    mean_square = jnp.sum(jnp.sum(sq[...], axis=0), axis=1, keepdims=True) / (2 * half * LANES * fsdps)
    factor = target_rms / jnp.sqrt(mean_square + 1e-06)
    slope = (outer_rate * (1.0 + outer_mu)) * factor

    outs = []
    for s, grads in ((1, gmine), (0, gother)):
        for c in range(chunks):
            if s == 0:
                third[c].wait_recv()
            grad = grads[part(c)].astype(jnp.float32)
            mv[s, part(c)] = mv[s, part(c)] + factor * grad
            pv[s, part(c)] = pv[s, part(c)] - slope * grad
            for v, out, sem in ((mv, newm_hbm, om_sem), (pv, newp_hbm, op_sem)):
                copy = pltpu.make_async_copy(
                    v.at[s, part(c)], out.at[piece(starts[s], c)], sem.at[s, c])
                copy.start()
                outs.append(copy)

    for copy in first + second + third:
        copy.wait_send()

    def told(d, carry):
        pltpu.make_async_remote_copy(
            sq.at[me], sq.at[me], s4.at[d], r4.at[me],
            device_id=sum_peer(d)[1], device_id_type=MESH).wait_send()
        return carry

    lax.fori_loop(1, sources, told, 0)
    for copy in outs:
        copy.wait()


def local(reps, fsdps, deltas, noise_first, params, momentum, noise_second):
    size = params.shape[0]
    total_rows = size // LANES
    half = total_rows // 2
    chunks = next(c for c in (4, 2, 1) if half % (16 * c) == 0)
    chips, sources = reps // 2, 2 * fsdps
    shape = (total_rows, LANES)
    f32, bf16 = jnp.float32, jnp.bfloat16
    dma = pltpu.SemaphoreType.DMA
    hbm = pl.BlockSpec(memory_space=pl.ANY)
    out = jax.ShapeDtypeStruct(shape, f32)
    new_params, new_momentum = pl.pallas_call(
        functools.partial(kernel, reps, fsdps, chunks),
        out_shape=(out, out),
        in_specs=[hbm] * 5,
        out_specs=(hbm, hbm),
        scratch_shapes=[
            pltpu.VMEM((2, half, LANES), f32),
            pltpu.VMEM((2, half, LANES), f32),
            pltpu.VMEM((half, LANES), f32),
            pltpu.VMEM((2, half, LANES), f32),
            pltpu.VMEM((2, half, LANES), f32),
            pltpu.VMEM((half, LANES), bf16),
            pltpu.VMEM((half, LANES), f32),
            pltpu.VMEM((half, LANES), bf16),
            pltpu.VMEM((chips, half, LANES), bf16),
            pltpu.VMEM((half, LANES), bf16),
            pltpu.VMEM((half, LANES), bf16),
            pltpu.VMEM((sources, 1, LANES), f32),
            dma((2, chunks)), dma((2, chunks)), dma, dma((2,)), dma((2,)),
            dma((2, chunks)), dma((2, chunks)),
            dma((chunks,)), dma((chunks,)),
            dma((chips, chunks)), dma((chips, chunks)),
            dma((chunks,)), dma((chunks,)),
            dma((sources,)), dma((sources,)),
        ],
        compiler_params=pltpu.CompilerParams(collective_id=0, has_side_effects=True),
        name="outer_step",
    )(deltas.reshape(shape), noise_first.reshape(shape), params.reshape(shape),
      momentum.reshape(shape), noise_second.reshape(shape))
    return new_params.reshape(size), new_momentum.reshape(size)


def solution(mesh):
    in_specs = (P("rep", "fsdp"), P("rep", "fsdp"), P("fsdp"), P("fsdp"), P("fsdp"))
    out_specs = (P("fsdp"), P("fsdp"))
    body = functools.partial(local, mesh.shape["rep"], mesh.shape["fsdp"])
    return jax.shard_map(body, mesh=mesh, in_specs=in_specs, out_specs=out_specs, check_vma=False)
```

time: 87.9 us -> 23.8 us (0.27)
  waiting for transfers between devices: 35.2 us -> 0 us
  blocking collectives: 22 us -> 0 us
  Pallas kernels: 0 us -> 20.3 us
  between operations: 14.9 us -> 0.65 us
  other arithmetic: 10.3 us -> 0 us
  local copies, waits for them, and re-layouts: 5.3 us -> 2.76 us
    psum x1 -> x0, waiting for transfers between devices: 35.1 us -> none  [local(): summed = lax.psum(own_terms.astype(jnp.bfloat16), 'rep').astype(jnp.float32)]
    psum x1 -> x0, blocking collectives: 22 us -> none  [local(): lax.psum(jnp.sum(outer_grad * outer_grad), 'fsdp') / full_count]
    pallas_call x0 -> x1, Pallas kernels: none -> 20.3 us  [local(): pl.pallas_call(functools.partial(kernel, reps, fsdps, chunks), out_shape=...]
    mul x8 -> x0, local copies, waits for them, and re-layouts: 4.33 us -> none  [the longest x4 2.16 us: quantize(): scaled = blocks * (LEVELS / ceiling)]
    abs x2 -> x0, other arithmetic: 3.63 us -> none  [quantize(): largest = jnp.max(jnp.abs(blocks), axis=1, keepdims=True)]
    unnamed x10 -> x4, local copies, waits for them, and re-layouts: 0.03 us -> 2.76 us
    convert_element_type x1 -> x0, other arithmetic: 2.04 us -> none  [local(): summed = lax.psum(own_terms.astype(jnp.bfloat16), 'rep').astype(jnp.float32)]
    reduce_sum x1 -> x0, other arithmetic: 1.92 us -> none  [local(): jnp.sum(outer_grad * outer_grad)]
  transfers between devices with their start and end apart: 1 -> 0, of which waited for: 1 -> 0; matrix products, arithmetic and copies ran while one was open for 0% -> 0% of each run, Pallas kernels for 0% -> 0%
where the time goes in v1:
time: 23.8 us; the launch traced here: 23.7 us
  Pallas kernels  20.3 us (85%)
  local copies, waits for them, and re-layouts  2.76 us (12%)
  between operations  0.65 us (3%)
    pallas_call x1, Pallas kernels, local(): pl.pallas_call(functools.partial(kernel, reps, fsdps, chunks), out_shape=...  20.3 us
    unnamed x4, local copies, waits for them, and re-layouts  2.76 us

profile of v1, /device:TPU:0, one launch (start us, length us, event | category | flops | bytes accessed | tf_op | source)
XLA Modules:
  0.0 23.7 jit_solution(3757492304161289341)
XLA Ops:
  0.6 20.3 %outer_step.1 = (f32[1024,128]{1,0:T(8,128)}, f32[1024,128]{1,0:T(8,128)}) custom-call(f32[1024,128]{1,0:T(8,128)} %bitcast.7, f32[1024,128]{1,0:T(8,128)} %bitcast.8, f32[1024,128]{1,0:T(8,128)} %bitcast.9, f32[1024,128]{1,0:T(8,128)} %bitcast.10, f32[1024,128]{1,0:T(8,128)} %bitcast.11), custom_call_target="tpu_custom_call" | custom-call | tf_op jit(solution)/shard_map/outer_step/pallas_call | solution.py:220
  20.9 0.0 copy-start
  20.9 1.9 %copy.9 = f32[131072]{0:T(1024)} copy(f32[131072]{0:T(1024)} %bitcast.13) | data formatting | bytes 1048576
  22.8 0.0 copy-done
  22.8 0.8 %copy.10 = f32[131072]{0:T(1024)} copy(f32[131072]{0:T(1024)S(1)} %bitcast.12) | data formatting | bytes 1048576
Async XLA Ops:
  20.9 1.9 %copy-start = (f32[1024,128]{1,0:T(8,128)S(1)}, f32[1024,128]{1,0:T(8,128)}, u32[]{:S(2)}) copy-start(f32[1024,128]{1,0:T(8,128)} %get-tuple-element.5) | copy-start | bytes 1572868

commit v2 on v1

--- a/solution.py
+++ b/solution.py
@@ -40,10 +40,9 @@
     return lower + jnp.where(values - lower > jitter * unit, unit, 0.0)
 
 
-def kernel(reps, fsdps, chunks, x_hbm, u_hbm, p_hbm, m_hbm, w_hbm, newp_hbm, newm_hbm,
-           xv, uv, wv, pv, mv, snd, own, got, pair, gmine, gother, sq,
-           x_sem, u_sem, w_sem, p_sem, m_sem, op_sem, om_sem,
-           s1, r1, s2, r2, s3, r3, s4, r4):
+def gather(reps, fsdps, chunks, x_hbm, u_hbm, p_hbm, m_hbm, w_hbm, pv, mv, grads, sq,
+           xv, uv, wv, snd, own, got, pair,
+           x_sem, u_sem, w_sem, p_sem, m_sem, s1, r1, s2, r2, s3, r3, s4, r4, hands):
     rep, fsdp = lax.axis_index("rep"), lax.axis_index("fsdp")
     core, chip = lax.rem(rep, 2), rep // 2
     partner = rep + 1 - 2 * core
@@ -64,11 +63,20 @@
     for d in range(1, chips):
         pl.semaphore_signal(barrier, inc=1, device_id=chip_peer(d)[1], device_id_type=MESH)
 
-    def greet(d, carry):
-        pl.semaphore_signal(barrier, inc=1, device_id=sum_peer(d)[1], device_id_type=MESH)
-        return carry
-
-    lax.fori_loop(1, sources, greet, 0)
+    bits = (sources - 1).bit_length()
+
+    def cube_peer(k):
+        other = me + (1 - 2 * lax.rem(me // 2**k, 2)) * 2**k
+        return (rep - core + lax.rem(other, 2), other // 2)
+
+    for k in range(bits):
+        pl.semaphore_signal(barrier, inc=1, device_id=cube_peer(k), device_id_type=MESH)
+
+    def pass_on(k):
+        pl.semaphore_signal(hands.at[k], inc=1, device_id=cube_peer(k), device_id_type=MESH)
+
+    def take_in(k):
+        pl.semaphore_wait(hands.at[k], 1)
 
     starts = ((1 - core) * half, core * half)
 
@@ -104,12 +112,13 @@
         u_in[0, c].wait()
         snd[part(c)] = quantize(xv[0, part(c)], uv[0, part(c)]).astype(jnp.bfloat16)
         if c == 0:
-            pl.semaphore_wait(barrier, chips - 1 + sources - 1)
+            pl.semaphore_wait(barrier, chips - 1 + bits)
         copy = pltpu.make_async_remote_copy(
             snd.at[part(c)], got.at[part(c)], s1.at[c], r1.at[c],
             device_id=(partner, fsdp), device_id_type=MESH)
         copy.start()
         first.append(copy)
+    pass_on(bits - 1)
     for c in range(chunks):
         x_in[1, c].wait()
         u_in[1, c].wait()
@@ -129,12 +138,18 @@
             second.append(copy)
 
     for s in (1, 0):
+        take_in(bits - 1) if s == 1 else None
+        pass_on(bits - 2) if s == 1 else None
         m_in[s].wait()
         p_in[s].wait()
         pv[s] = pv[s] - (outer_rate * outer_mu * outer_mu) * mv[s]
         mv[s] = outer_mu * mv[s]
 
     w_in.wait()
+    for k in range(bits - 2, -1, -1):
+        take_in(k)
+        if k:
+            pass_on(k - 1)
     third = []
     squares = jnp.zeros((8, LANES), jnp.float32)
     for c in range(chunks):
@@ -148,9 +163,9 @@
         for k in range(1, chips):
             total = total + pair[k, part(c)].astype(jnp.float32)
         grad = quantize(total / reps, wv[part(c)])
-        gmine[part(c)] = grad.astype(jnp.bfloat16)
+        grads[1, part(c)] = grad.astype(jnp.bfloat16)
         copy = pltpu.make_async_remote_copy(
-            gmine.at[part(c)], gother.at[part(c)], s3.at[c], r3.at[c],
+            grads.at[1, part(c)], grads.at[0, part(c)], s3.at[c], r3.at[c],
             device_id=(partner, fsdp), device_id_type=MESH)
         copy.start()
         third.append(copy)
@@ -174,24 +189,8 @@
         return carry
 
     lax.fori_loop(1, sources, hear, 0)
-    mean_square = jnp.sum(jnp.sum(sq[...], axis=0), axis=1, keepdims=True) / (2 * half * LANES * fsdps)
-    factor = target_rms / jnp.sqrt(mean_square + 1e-06)
-    slope = (outer_rate * (1.0 + outer_mu)) * factor
-
-    outs = []
-    for s, grads in ((1, gmine), (0, gother)):
-        for c in range(chunks):
-            if s == 0:
-                third[c].wait_recv()
-            grad = grads[part(c)].astype(jnp.float32)
-            mv[s, part(c)] = mv[s, part(c)] + factor * grad
-            pv[s, part(c)] = pv[s, part(c)] - slope * grad
-            for v, out, sem in ((mv, newm_hbm, om_sem), (pv, newp_hbm, op_sem)):
-                copy = pltpu.make_async_copy(
-                    v.at[s, part(c)], out.at[piece(starts[s], c)], sem.at[s, c])
-                copy.start()
-                outs.append(copy)
-
+    for copy in third:
+        copy.wait_recv()
     for copy in first + second + third:
         copy.wait_send()
 
@@ -202,6 +201,27 @@
         return carry
 
     lax.fori_loop(1, sources, told, 0)
+
+
+def finish(count, chunks, pv, mv, grads, sq, newp_hbm, newm_hbm, op, om, op_sem, om_sem):
+    core = lax.rem(lax.axis_index("rep"), 2)
+    half = pv.shape[1]
+    rows = half // chunks
+    mean_square = jnp.sum(jnp.sum(sq[...], axis=0), axis=1, keepdims=True) / count
+    factor = target_rms / jnp.sqrt(mean_square + 1e-06)
+    slope = (outer_rate * (1.0 + outer_mu)) * factor
+    outs = []
+    for s, start in ((1, core * half), (0, (1 - core) * half)):
+        for c in range(chunks):
+            part = pl.ds(c * rows, rows)
+            grad = grads[s, part].astype(jnp.float32)
+            om[s, part] = mv[s, part] + factor * grad
+            op[s, part] = pv[s, part] - slope * grad
+            piece = pl.ds(pl.multiple_of(start + c * rows, rows), rows)
+            for v, out, sem in ((om, newm_hbm, om_sem), (op, newp_hbm, op_sem)):
+                copy = pltpu.make_async_copy(v.at[s, part], out.at[piece], sem.at[s, c])
+                copy.start()
+                outs.append(copy)
     for copy in outs:
         copy.wait()
 
@@ -210,42 +230,49 @@
     size = params.shape[0]
     total_rows = size // LANES
     half = total_rows // 2
-    chunks = next(c for c in (4, 2, 1) if half % (16 * c) == 0)
+    chunks = next(c for c in (2, 1) if half % (16 * c) == 0)
     chips, sources = reps // 2, 2 * fsdps
     shape = (total_rows, LANES)
     f32, bf16 = jnp.float32, jnp.bfloat16
     dma = pltpu.SemaphoreType.DMA
     hbm = pl.BlockSpec(memory_space=pl.ANY)
+    vmem = pl.BlockSpec(memory_space=pltpu.VMEM)
     out = jax.ShapeDtypeStruct(shape, f32)
-    new_params, new_momentum = pl.pallas_call(
-        functools.partial(kernel, reps, fsdps, chunks),
-        out_shape=(out, out),
+    halves = (2, half, LANES)
+    parts = pl.pallas_call(
+        functools.partial(gather, reps, fsdps, chunks),
+        out_shape=(pltpu.VMEM(halves, f32), pltpu.VMEM(halves, f32),
+                   pltpu.VMEM(halves, bf16), pltpu.VMEM((sources, 1, LANES), f32)),
         in_specs=[hbm] * 5,
-        out_specs=(hbm, hbm),
+        out_specs=(vmem,) * 4,
         scratch_shapes=[
-            pltpu.VMEM((2, half, LANES), f32),
-            pltpu.VMEM((2, half, LANES), f32),
+            pltpu.VMEM(halves, f32),
+            pltpu.VMEM(halves, f32),
             pltpu.VMEM((half, LANES), f32),
-            pltpu.VMEM((2, half, LANES), f32),
-            pltpu.VMEM((2, half, LANES), f32),
             pltpu.VMEM((half, LANES), bf16),
             pltpu.VMEM((half, LANES), f32),
             pltpu.VMEM((half, LANES), bf16),
             pltpu.VMEM((chips, half, LANES), bf16),
-            pltpu.VMEM((half, LANES), bf16),
-            pltpu.VMEM((half, LANES), bf16),
-            pltpu.VMEM((sources, 1, LANES), f32),
             dma((2, chunks)), dma((2, chunks)), dma, dma((2,)), dma((2,)),
-            dma((2, chunks)), dma((2, chunks)),
             dma((chunks,)), dma((chunks,)),
             dma((chips, chunks)), dma((chips, chunks)),
             dma((chunks,)), dma((chunks,)),
             dma((sources,)), dma((sources,)),
+            pltpu.SemaphoreType.REGULAR(((sources - 1).bit_length(),)),
         ],
         compiler_params=pltpu.CompilerParams(collective_id=0, has_side_effects=True),
-        name="outer_step",
+        name="gather_step",
     )(deltas.reshape(shape), noise_first.reshape(shape), params.reshape(shape),
       momentum.reshape(shape), noise_second.reshape(shape))
+    new_params, new_momentum = pl.pallas_call(
+        functools.partial(finish, size * fsdps, chunks),
+        out_shape=(out, out),
+        in_specs=[vmem] * 4,
+        out_specs=(hbm, hbm),
+        scratch_shapes=[pltpu.VMEM(halves, f32), pltpu.VMEM(halves, f32),
+                        dma((2, chunks)), dma((2, chunks))],
+        name="finish_step",
+    )(*[pltpu.with_memory_space_constraint(p, pltpu.VMEM) for p in parts])
     return new_params.reshape(size), new_momentum.reshape(size)
 
 

time: 23.8 us -> 19.3 us (0.81)
  local copies, waits for them, and re-layouts: 2.76 us -> 0 us
  Pallas kernels: 20.3 us -> 18.5 us
    unnamed x4 -> x0, local copies, waits for them, and re-layouts: 2.76 us -> none
    pallas_call x1 -> x2, Pallas kernels: 20.3 us -> 18.5 us  [the longest x1 17.4 us: local(): pl.pallas_call(functools.partial(gather, reps, fsdps, chunks), out_shape=...]
where the time goes in v2:
time: 19.3 us; the launch traced here: 19.1 us
  Pallas kernels  18.5 us (96%)
  between operations  0.64 us (3%)
    pallas_call x1, Pallas kernels, local(): pl.pallas_call(functools.partial(gather, reps, fsdps, chunks), out_shape=...  17.4 us
    pallas_call x1, Pallas kernels, local(): pl.pallas_call(functools.partial(finish, size * fsdps, chunks), out_shape...  1.15 us

profile of v2, /device:TPU:0, one launch (start us, length us, event | category | flops | bytes accessed | tf_op | source)
XLA Modules:
  0.0 19.1 jit_solution(4597212286622908672)
XLA Ops:
  0.6 17.4 %gather_step.1 = (f32[2,512,128]{2,1,0:T(8,128)S(1)}, f32[2,512,128]{2,1,0:T(8,128)S(1)}, bf16[2,512,128]{2,1,0:T(8,128)(2,1)S(1)}, f32[16,1,128]{2,1,0:T(1,128)S(1)}) custom-call(f32[1024,128]{1,0:T(8,128)} %bitcast.7, f32[1024,128]{1,0:T(8,128)} %bitcast.8, f32[1024,128]{1,0:T(8,128)} %bitcast.9, f32[1024,128]{1,0:T(8,128)} %bitcast.10, f32[1024,128]{1,0:T(8,128)} %bitcast.11), custom_call_target="tpu_custom_call" | custom-call | tf_op jit(solution)/shard_map/gather_step/pallas_call | solution.py:242
  18.0 1.2 %finish_step.1 = (f32[1024,128]{1,0:T(8,128)}, f32[1024,128]{1,0:T(8,128)}) custom-call(f32[2,512,128]{2,1,0:T(8,128)S(1)} %get-tuple-element.8.pv, f32[2,512,128]{2,1,0:T(8,128)S(1)} %get-tuple-element.9.mv, bf16[2,512,128]{2,1,0:T(8,128)(2,1)S(1)} %get-tuple-element.10.grads, f32[16,1,128]{2,1,0:T(1,128)S(1)} %get-tuple-element.11.sq), custom_call_target="tpu_custom_call" | custom-call | tf_op jit(solution)/shard_map/finish_step/pallas_call | solution.py:267

commit v3 on v2

--- a/solution.py
+++ b/solution.py
@@ -173,34 +173,19 @@
 
     sq[me] = jnp.sum(squares, axis=0, keepdims=True)
 
-    def tell(d, carry):
+    for d in range(1, sources):
         pltpu.make_async_remote_copy(
-            sq.at[me], sq.at[me], s4.at[d], r4.at[me],
+            sq.at[me], sq.at[me], s4, r4,
             device_id=sum_peer(d)[1], device_id_type=MESH).start()
-        return carry
-
-    lax.fori_loop(1, sources, tell, 0)
-
-    def hear(d, carry):
-        other, where = sum_peer(d)
-        pltpu.make_async_remote_copy(
-            sq.at[other], sq.at[other], s4.at[d], r4.at[other],
-            device_id=where, device_id_type=MESH).wait_recv()
-        return carry
-
-    lax.fori_loop(1, sources, hear, 0)
+    others = sq.at[pl.ds(0, sources - 1)]
+    sums = pltpu.make_async_remote_copy(
+        others, others, s4, r4, device_id=(partner, fsdp), device_id_type=MESH)
     for copy in third:
         copy.wait_recv()
     for copy in first + second + third:
         copy.wait_send()
-
-    def told(d, carry):
-        pltpu.make_async_remote_copy(
-            sq.at[me], sq.at[me], s4.at[d], r4.at[me],
-            device_id=sum_peer(d)[1], device_id_type=MESH).wait_send()
-        return carry
-
-    lax.fori_loop(1, sources, told, 0)
+    sums.wait_recv()
+    sums.wait_send()
 
 
 def finish(count, chunks, pv, mv, grads, sq, newp_hbm, newm_hbm, op, om, op_sem, om_sem):
@@ -257,7 +242,7 @@
             dma((chunks,)), dma((chunks,)),
             dma((chips, chunks)), dma((chips, chunks)),
             dma((chunks,)), dma((chunks,)),
-            dma((sources,)), dma((sources,)),
+            dma, dma,
             pltpu.SemaphoreType.REGULAR(((sources - 1).bit_length(),)),
         ],
         compiler_params=pltpu.CompilerParams(collective_id=0, has_side_effects=True),

time: 19.3 us -> 18.8 us (0.974)
  Pallas kernels: 18.5 us -> 18 us
    pallas_call x1, Pallas kernels: 17.4 us -> 16.9 us  [local(): pl.pallas_call(functools.partial(gather, reps, fsdps, chunks), out_shape=...]
where the time goes in v3:
time: 18.8 us; the launch traced here: 18.7 us
  Pallas kernels  18 us (96%)
  between operations  0.64 us (3%)
    pallas_call x1, Pallas kernels, local(): pl.pallas_call(functools.partial(gather, reps, fsdps, chunks), out_shape=...  16.9 us
    pallas_call x1, Pallas kernels, local(): pl.pallas_call(functools.partial(finish, size * fsdps, chunks), out_shape...  1.15 us

profile of v3, /device:TPU:0, one launch (start us, length us, event | category | flops | bytes accessed | tf_op | source)
XLA Modules:
  0.0 18.7 jit_solution(12869590586132258885)
XLA Ops:
  0.6 16.9 %gather_step.1 = (f32[2,512,128]{2,1,0:T(8,128)S(1)}, f32[2,512,128]{2,1,0:T(8,128)S(1)}, bf16[2,512,128]{2,1,0:T(8,128)(2,1)S(1)}, f32[16,1,128]{2,1,0:T(1,128)S(1)}) custom-call(f32[1024,128]{1,0:T(8,128)} %bitcast.7, f32[1024,128]{1,0:T(8,128)} %bitcast.8, f32[1024,128]{1,0:T(8,128)} %bitcast.9, f32[1024,128]{1,0:T(8,128)} %bitcast.10, f32[1024,128]{1,0:T(8,128)} %bitcast.11), custom_call_target="tpu_custom_call" | custom-call | tf_op jit(solution)/shard_map/gather_step/pallas_call | solution.py:227
  17.5 1.2 %finish_step.1 = (f32[1024,128]{1,0:T(8,128)}, f32[1024,128]{1,0:T(8,128)}) custom-call(f32[2,512,128]{2,1,0:T(8,128)S(1)} %get-tuple-element.8.pv, f32[2,512,128]{2,1,0:T(8,128)S(1)} %get-tuple-element.9.mv, bf16[2,512,128]{2,1,0:T(8,128)(2,1)S(1)} %get-tuple-element.10.grads, f32[16,1,128]{2,1,0:T(1,128)S(1)} %get-tuple-element.11.sq), custom_call_target="tpu_custom_call" | custom-call | tf_op jit(solution)/shard_map/finish_step/pallas_call | solution.py:252

commit v4 on v3

--- a/solution.py
+++ b/solution.py
@@ -18,22 +18,13 @@
 outer_mu = 0.9
 
 
-def block_max(values):
-    lane = lax.broadcasted_iota(jnp.int32, values.shape, 1)
-    largest = jnp.abs(values)
-    step = 1
-    while step < BLOCK:
-        ahead = pltpu.roll(largest, LANES - step, 1)
-        behind = pltpu.roll(largest, step, 1)
-        largest = jnp.maximum(largest, jnp.where((lane & step) != 0, behind, ahead))
-        step *= 2
-    return largest
-
-
 def quantize(values, jitter):
-    largest = jnp.maximum(block_max(values), SMALLEST)
+    rows = values.shape[0]
+    turned = jnp.abs(values).T.reshape(LANES // BLOCK, BLOCK, rows)
+    largest = jnp.maximum(jnp.max(turned, axis=1, keepdims=True), SMALLEST)
     spread = (largest * UNDER) * ((2.0**24 + 2.0) / LEVELS)
     unit = spread - spread * UNDER
+    unit = jnp.broadcast_to(unit, turned.shape).reshape(LANES, rows).T
     magic = unit * (1.5 * 2.0**23)
     near = (values + magic) - magic
     lower = jnp.where(near > values, near - unit, near)

time: 18.8 us -> 17.8 us (0.947)
  Pallas kernels: 18 us -> 17 us
    pallas_call x1, Pallas kernels: 16.9 us -> 15.9 us  [local(): pl.pallas_call(functools.partial(gather, reps, fsdps, chunks), out_shape=...]
where the time goes in v4:
time: 17.8 us; the launch traced here: 17.7 us
  Pallas kernels  17 us (96%)
  between operations  0.64 us (4%)
    pallas_call x1, Pallas kernels, local(): pl.pallas_call(functools.partial(gather, reps, fsdps, chunks), out_shape=...  15.9 us
    pallas_call x1, Pallas kernels, local(): pl.pallas_call(functools.partial(finish, size * fsdps, chunks), out_shape...  1.15 us

profile of v4, /device:TPU:0, one launch (start us, length us, event | category | flops | bytes accessed | tf_op | source)
XLA Modules:
  0.0 17.7 jit_solution(7378384024185831047)
XLA Ops:
  0.6 15.9 %gather_step.1 = (f32[2,512,128]{2,1,0:T(8,128)S(1)}, f32[2,512,128]{2,1,0:T(8,128)S(1)}, bf16[2,512,128]{2,1,0:T(8,128)(2,1)S(1)}, f32[16,1,128]{2,1,0:T(1,128)S(1)}) custom-call(f32[1024,128]{1,0:T(8,128)} %bitcast.7, f32[1024,128]{1,0:T(8,128)} %bitcast.8, f32[1024,128]{1,0:T(8,128)} %bitcast.9, f32[1024,128]{1,0:T(8,128)} %bitcast.10, f32[1024,128]{1,0:T(8,128)} %bitcast.11), custom_call_target="tpu_custom_call" | custom-call | tf_op jit(solution)/shard_map/gather_step/pallas_call | solution.py:218
  16.5 1.2 %finish_step.1 = (f32[1024,128]{1,0:T(8,128)}, f32[1024,128]{1,0:T(8,128)}) custom-call(f32[2,512,128]{2,1,0:T(8,128)S(1)} %get-tuple-element.8.pv, f32[2,512,128]{2,1,0:T(8,128)S(1)} %get-tuple-element.9.mv, bf16[2,512,128]{2,1,0:T(8,128)(2,1)S(1)} %get-tuple-element.10.grads, f32[16,1,128]{2,1,0:T(1,128)S(1)} %get-tuple-element.11.sq), custom_call_target="tpu_custom_call" | custom-call | tf_op jit(solution)/shard_map/finish_step/pallas_call | solution.py:243

commit v5 on v4

--- a/solution.py
+++ b/solution.py
@@ -32,8 +32,8 @@
 
 
 def gather(reps, fsdps, chunks, x_hbm, u_hbm, p_hbm, m_hbm, w_hbm, pv, mv, grads, sq,
-           xv, uv, wv, snd, own, got, pair,
-           x_sem, u_sem, w_sem, p_sem, m_sem, s1, r1, s2, r2, s3, r3, s4, r4, hands):
+           xv, uv, wv, snd, own, got, pair, raw,
+           x_sem, u_sem, w_sem, p_sem, m_sem, s1, r1, s2, r2, s3, r3, s4, r4, s5, r5, hands):
     rep, fsdp = lax.axis_index("rep"), lax.axis_index("fsdp")
     core, chip = lax.rem(rep, 2), rep // 2
     partner = rep + 1 - 2 * core
@@ -52,7 +52,9 @@
 
     barrier = pltpu.get_barrier_semaphore()
     for d in range(1, chips):
-        pl.semaphore_signal(barrier, inc=1, device_id=chip_peer(d)[1], device_id_type=MESH)
+        other, where = chip_peer(d)
+        pl.semaphore_signal(barrier, inc=1, device_id=where, device_id_type=MESH)
+        pl.semaphore_signal(barrier, inc=1, device_id=(2 * other + 1 - core, fsdp), device_id_type=MESH)
 
     bits = (sources - 1).bit_length()
 
@@ -97,27 +99,46 @@
         m_in[s].start()
         p_in[s].start()
 
+    straight = []
+
+    def send_straight(source, k, cores):
+        copy = pltpu.make_async_remote_copy(
+            source, raw.at[rep], s5.at[len(straight)], r5.at[rep],
+            device_id=(2 * k + cores, fsdp), device_id_type=MESH)
+        copy.start()
+        straight.append(copy)
+
+    x_in[0, 0].wait()
+    u_in[0, 0].wait()
+    snd[part(0)] = quantize(xv[0, part(0)], uv[0, part(0)]).astype(jnp.bfloat16)
+    pl.semaphore_wait(barrier, 2 * (chips - 1) + bits)
+    for d in range(chips):
+        send_straight(snd.at[part(0)], lax.rem(chip + d, chips), 1 - core)
+    x_in[1, 0].wait()
+    u_in[1, 0].wait()
+    raw[rep] = quantize(xv[1, part(0)], uv[1, part(0)]).astype(jnp.bfloat16)
+    for d in range(1, chips):
+        send_straight(raw.at[rep], lax.rem(chip + d, chips), core)
+
     first = []
-    for c in range(chunks):
+    for c in range(1, chunks):
         x_in[0, c].wait()
         u_in[0, c].wait()
         snd[part(c)] = quantize(xv[0, part(c)], uv[0, part(c)]).astype(jnp.bfloat16)
-        if c == 0:
-            pl.semaphore_wait(barrier, chips - 1 + bits)
         copy = pltpu.make_async_remote_copy(
             snd.at[part(c)], got.at[part(c)], s1.at[c], r1.at[c],
             device_id=(partner, fsdp), device_id_type=MESH)
         copy.start()
         first.append(copy)
     pass_on(bits - 1)
-    for c in range(chunks):
+    for c in range(1, chunks):
         x_in[1, c].wait()
         u_in[1, c].wait()
         own[part(c)] = quantize(xv[1, part(c)], uv[1, part(c)])
 
     second = []
-    for c in range(chunks):
-        first[c].wait_recv()
+    for c in range(1, chunks):
+        first[c - 1].wait_recv()
         both = own[part(c)] + got[part(c)].astype(jnp.float32)
         pair[chip, part(c)] = both.astype(jnp.bfloat16)
         for d in range(1, chips):
@@ -137,22 +158,28 @@
         mv[s] = outer_mu * mv[s]
 
     w_in.wait()
-    for k in range(bits - 2, -1, -1):
-        take_in(k)
-        if k:
-            pass_on(k - 1)
     third = []
     squares = jnp.zeros((8, LANES), jnp.float32)
     for c in range(chunks):
-        for d in range(1, chips):
-            other, where = chip_peer(d)
-            pltpu.make_async_remote_copy(
-                pair.at[other, part(c)], pair.at[other, part(c)],
-                s2.at[d, c], r2.at[other, c],
-                device_id=where, device_id_type=MESH).wait_recv()
-        total = pair[0, part(c)].astype(jnp.float32)
-        for k in range(1, chips):
-            total = total + pair[k, part(c)].astype(jnp.float32)
+        if c == 0:
+            for d in range(1, reps):
+                source = lax.rem(rep + d, reps)
+                pltpu.make_async_remote_copy(
+                    raw.at[source], raw.at[source], s5.at[0], r5.at[source],
+                    device_id=(source, fsdp), device_id_type=MESH).wait_recv()
+            total = raw[0].astype(jnp.float32)
+            for k in range(1, reps):
+                total = total + raw[k].astype(jnp.float32)
+        else:
+            for d in range(1, chips):
+                other, where = chip_peer(d)
+                pltpu.make_async_remote_copy(
+                    pair.at[other, part(c)], pair.at[other, part(c)],
+                    s2.at[d, c], r2.at[other, c],
+                    device_id=where, device_id_type=MESH).wait_recv()
+            total = pair[0, part(c)].astype(jnp.float32)
+            for k in range(1, chips):
+                total = total + pair[k, part(c)].astype(jnp.float32)
         grad = quantize(total / reps, wv[part(c)])
         grads[1, part(c)] = grad.astype(jnp.bfloat16)
         copy = pltpu.make_async_remote_copy(
@@ -160,6 +187,11 @@
             device_id=(partner, fsdp), device_id_type=MESH)
         copy.start()
         third.append(copy)
+        if c == 0:
+            for k in range(bits - 2, -1, -1):
+                take_in(k)
+                if k:
+                    pass_on(k - 1)
         squares = squares + jnp.sum((grad * grad).reshape(-1, 8, LANES), axis=0)
 
     sq[me] = jnp.sum(squares, axis=0, keepdims=True)
@@ -173,7 +205,7 @@
         others, others, s4, r4, device_id=(partner, fsdp), device_id_type=MESH)
     for copy in third:
         copy.wait_recv()
-    for copy in first + second + third:
+    for copy in straight + first + second + third:
         copy.wait_send()
     sums.wait_recv()
     sums.wait_send()
@@ -206,7 +238,7 @@
     size = params.shape[0]
     total_rows = size // LANES
     half = total_rows // 2
-    chunks = next(c for c in (2, 1) if half % (16 * c) == 0)
+    chunks = next(c for c in (4, 2, 1) if half % (16 * c) == 0)
     chips, sources = reps // 2, 2 * fsdps
     shape = (total_rows, LANES)
     f32, bf16 = jnp.float32, jnp.bfloat16
@@ -229,11 +261,12 @@
             pltpu.VMEM((half, LANES), f32),
             pltpu.VMEM((half, LANES), bf16),
             pltpu.VMEM((chips, half, LANES), bf16),
+            pltpu.VMEM((reps, half // chunks, LANES), bf16),
             dma((2, chunks)), dma((2, chunks)), dma, dma((2,)), dma((2,)),
             dma((chunks,)), dma((chunks,)),
             dma((chips, chunks)), dma((chips, chunks)),
             dma((chunks,)), dma((chunks,)),
-            dma, dma,
+            dma, dma, dma((reps,)), dma((reps,)),
             pltpu.SemaphoreType.REGULAR(((sources - 1).bit_length(),)),
         ],
         compiler_params=pltpu.CompilerParams(collective_id=0, has_side_effects=True),

time: 17.8 us -> 17.7 us (level)
  no operation moved by 1% of the time
where the time goes in v5:
time: 17.7 us; the launch traced here: 17.5 us
  Pallas kernels  16.9 us (95%)
  between operations  0.64 us (4%)
    pallas_call x1, Pallas kernels, local(): pl.pallas_call(functools.partial(gather, reps, fsdps, chunks), out_shape=...  15.7 us
    pallas_call x1, Pallas kernels, local(): pl.pallas_call(functools.partial(finish, size * fsdps, chunks), out_shape...  1.21 us

profile of v5, /device:TPU:0, one launch (start us, length us, event | category | flops | bytes accessed | tf_op | source)
XLA Modules:
  0.0 17.5 jit_solution(15572907750115032710)
XLA Ops:
  0.6 15.7 %gather_step.1 = (f32[2,512,128]{2,1,0:T(8,128)S(1)}, f32[2,512,128]{2,1,0:T(8,128)S(1)}, bf16[2,512,128]{2,1,0:T(8,128)(2,1)S(1)}, f32[16,1,128]{2,1,0:T(1,128)S(1)}) custom-call(f32[1024,128]{1,0:T(8,128)} %bitcast.7, f32[1024,128]{1,0:T(8,128)} %bitcast.8, f32[1024,128]{1,0:T(8,128)} %bitcast.9, f32[1024,128]{1,0:T(8,128)} %bitcast.10, f32[1024,128]{1,0:T(8,128)} %bitcast.11), custom_call_target="tpu_custom_call" | custom-call | tf_op jit(solution)/shard_map/gather_step/pallas_call | solution.py:250
  16.3 1.2 %finish_step.1 = (f32[1024,128]{1,0:T(8,128)}, f32[1024,128]{1,0:T(8,128)}) custom-call(f32[2,512,128]{2,1,0:T(8,128)S(1)} %get-tuple-element.8.pv, f32[2,512,128]{2,1,0:T(8,128)S(1)} %get-tuple-element.9.mv, bf16[2,512,128]{2,1,0:T(8,128)(2,1)S(1)} %get-tuple-element.10.grads, f32[16,1,128]{2,1,0:T(1,128)S(1)} %get-tuple-element.11.sq), custom_call_target="tpu_custom_call" | custom-call | tf_op jit(solution)/shard_map/finish_step/pallas_call | solution.py:276

commit v6 on v4

--- a/solution.py
+++ b/solution.py
@@ -32,7 +32,7 @@
 
 
 def gather(reps, fsdps, chunks, x_hbm, u_hbm, p_hbm, m_hbm, w_hbm, pv, mv, grads, sq,
-           xv, uv, wv, snd, own, got, pair,
+           xv, uv, wv, snd, got, pair,
            x_sem, u_sem, w_sem, p_sem, m_sem, s1, r1, s2, r2, s3, r3, s4, r4, hands):
     rep, fsdp = lax.axis_index("rep"), lax.axis_index("fsdp")
     core, chip = lax.rem(rep, 2), rep // 2
@@ -110,15 +110,13 @@
         copy.start()
         first.append(copy)
     pass_on(bits - 1)
+    second = []
     for c in range(chunks):
         x_in[1, c].wait()
         u_in[1, c].wait()
-        own[part(c)] = quantize(xv[1, part(c)], uv[1, part(c)])
-
-    second = []
-    for c in range(chunks):
+        own = quantize(xv[1, part(c)], uv[1, part(c)])
         first[c].wait_recv()
-        both = own[part(c)] + got[part(c)].astype(jnp.float32)
+        both = own + got[part(c)].astype(jnp.float32)
         pair[chip, part(c)] = both.astype(jnp.bfloat16)
         for d in range(1, chips):
             copy = pltpu.make_async_remote_copy(
@@ -137,10 +135,6 @@
         mv[s] = outer_mu * mv[s]
 
     w_in.wait()
-    for k in range(bits - 2, -1, -1):
-        take_in(k)
-        if k:
-            pass_on(k - 1)
     third = []
     squares = jnp.zeros((8, LANES), jnp.float32)
     for c in range(chunks):
@@ -160,6 +154,11 @@
             device_id=(partner, fsdp), device_id_type=MESH)
         copy.start()
         third.append(copy)
+        if c == 0:
+            for k in range(bits - 2, -1, -1):
+                take_in(k)
+                if k:
+                    pass_on(k - 1)
         squares = squares + jnp.sum((grad * grad).reshape(-1, 8, LANES), axis=0)
 
     sq[me] = jnp.sum(squares, axis=0, keepdims=True)
@@ -226,7 +225,6 @@
             pltpu.VMEM(halves, f32),
             pltpu.VMEM((half, LANES), f32),
             pltpu.VMEM((half, LANES), bf16),
-            pltpu.VMEM((half, LANES), f32),
             pltpu.VMEM((half, LANES), bf16),
             pltpu.VMEM((chips, half, LANES), bf16),
             dma((2, chunks)), dma((2, chunks)), dma, dma((2,)), dma((2,)),

time: 17.8 us -> 17.8 us (level)
  no operation moved by 1% of the time
where the time goes in v6:
time: 17.8 us; the launch traced here: 17.7 us
  Pallas kernels  17 us (96%)
  between operations  0.64 us (4%)
    pallas_call x1, Pallas kernels, local(): pl.pallas_call(functools.partial(gather, reps, fsdps, chunks), out_shape=...  15.9 us
    pallas_call x1, Pallas kernels, local(): pl.pallas_call(functools.partial(finish, size * fsdps, chunks), out_shape...  1.15 us

profile of v6, /device:TPU:0, one launch (start us, length us, event | category | flops | bytes accessed | tf_op | source)
XLA Modules:
  0.0 17.7 jit_solution(14701409854705436690)
XLA Ops:
  0.6 15.9 %gather_step.1 = (f32[2,512,128]{2,1,0:T(8,128)S(1)}, f32[2,512,128]{2,1,0:T(8,128)S(1)}, bf16[2,512,128]{2,1,0:T(8,128)(2,1)S(1)}, f32[16,1,128]{2,1,0:T(1,128)S(1)}) custom-call(f32[1024,128]{1,0:T(8,128)} %bitcast.7, f32[1024,128]{1,0:T(8,128)} %bitcast.8, f32[1024,128]{1,0:T(8,128)} %bitcast.9, f32[1024,128]{1,0:T(8,128)} %bitcast.10, f32[1024,128]{1,0:T(8,128)} %bitcast.11), custom_call_target="tpu_custom_call" | custom-call | tf_op jit(solution)/shard_map/gather_step/pallas_call | solution.py:217
  16.5 1.2 %finish_step.1 = (f32[1024,128]{1,0:T(8,128)}, f32[1024,128]{1,0:T(8,128)}) custom-call(f32[2,512,128]{2,1,0:T(8,128)S(1)} %get-tuple-element.8.pv, f32[2,512,128]{2,1,0:T(8,128)S(1)} %get-tuple-element.9.mv, bf16[2,512,128]{2,1,0:T(8,128)(2,1)S(1)} %get-tuple-element.10.grads, f32[16,1,128]{2,1,0:T(1,128)S(1)} %get-tuple-element.11.sq), custom_call_target="tpu_custom_call" | custom-call | tf_op jit(solution)/shard_map/finish_step/pallas_call | solution.py:241
